TPU v7x, 256 devices: a whole 4x4x8 slice. The times are simulated.
256 devices in a mesh: src: 16 (over y_lo, x, core), rec: 16 (over y_hi, z).
Axes of the slice: x: 4, y: 4 (y_hi: 2, y_lo: 2; y = y_hi * 2 + y_lo), z: 8, core: 2. Of those that a mesh axis runs over, the one named last changes fastest.
Arguments:
- kernel: bfloat16 [2, 32, 4096, 4096], P(None, None, 'src', 'rec'), may hold values from -0.09375 to 0.09375
- focusing: float32 [64, 4096, 128], P(None, ('rec', 'src')), may hold values from -6 to 6
- first_arrival: float32 [64, 4096, 128], P(None, ('rec', 'src')), may hold values from -6 to 6
- onset: int32 [64, 4096], replicated, may hold values from 32 to 127
Outputs:
- upgoing: float32 [64, 4096, 128], P(None, ('src', 'rec'))
- downgoing: float32 [64, 4096, 128], P(None, ('rec', 'src'))
All inputs are finite; a program needn't handle non-finite values.
Results may differ from a plain program's by a relative error of at most 0.0029.
Values may be sent and summed in bfloat16 or wider, within the bound.
No kernel may reach another device: no remote copies, remote signals or barrier semaphores. Data moves between devices by JAX's collectives and lax.ppermute only.
A program may use at most 128 MiB of HBM per device.

v0:
```python
import jax
import jax.numpy as jnp
from jax import lax
from jax.sharding import PartitionSpec as P

HIGH = lax.Precision.HIGHEST


def tables(count, samples, flipped):
    steps = jnp.arange(samples, dtype=jnp.int32)
    if flipped:
        steps = samples - 1 - steps
    waves = jnp.arange(count, dtype=jnp.int32) + 1
    turns = waves[:, None] * steps[None, :] % samples
    angle = turns.astype(jnp.float32) * (2.0 * jnp.pi / samples)
    return (jnp.cos(angle), jnp.sin(angle))


def spectra(traces, cosine, sine):
    real_part = jnp.einsum("pnt,kt->kpn", traces, cosine, precision=HIGH)
    imag_part = -jnp.einsum("pnt,kt->kpn", traces, sine, precision=HIGH)
    return jnp.stack([real_part, imag_part]).astype(jnp.bfloat16)


def synth(stacked, cosine, sine, samples):
    first = jnp.einsum("kpn,kt->pnt", stacked[0], cosine, precision=HIGH)
    second = jnp.einsum("kpn,kt->pnt", stacked[1], sine, precision=HIGH)
    return 2.0 / samples * (first - second)


def onset_masked(values, onset, start, width):
    limits = lax.dynamic_slice_in_dim(onset, start, width, 1)
    times = jnp.arange(values.shape[2], dtype=jnp.int32)
    return times[None, None, :] < limits[:, :, None]


def per_device(kernel, focusing, first_arrival, onset):
    samples = focusing.shape[2]
    count = kernel.shape[1]
    width = focusing.shape[1]
    n_src = lax.axis_size("src")
    n_rec = lax.axis_size("rec")
    src_idx = lax.axis_index("src")
    rec_idx = lax.axis_index("rec")
    cosine, sine = tables(count, samples, False)
    rcosine, rsine = tables(count, samples, True)
    traces = lax.all_gather(focusing, "src", axis=1, tiled=True)
    wavefield_spectrum = spectra(traces, cosine, sine)
    kernel_real = kernel[0]
    kernel_imaginary = kernel[1]
    conv_re = jnp.einsum(
        "hoy,hny->hon", wavefield_spectrum[0], kernel_real, preferred_element_type=jnp.float32
    ) - jnp.einsum(
        "hoy,hny->hon", wavefield_spectrum[1], kernel_imaginary, preferred_element_type=jnp.float32
    )
    conv_im = jnp.einsum(
        "hoy,hny->hon", wavefield_spectrum[0], kernel_imaginary, preferred_element_type=jnp.float32
    ) + jnp.einsum(
        "hoy,hny->hon", wavefield_spectrum[1], kernel_real, preferred_element_type=jnp.float32
    )
    conv = jnp.stack([conv_re, conv_im])
    share = lax.psum_scatter(conv, "rec", scatter_dimension=3, tiled=True)
    start = (src_idx * n_rec + rec_idx) * width
    traces_up = synth(share, cosine, sine, samples)
    upgoing = jnp.where(onset_masked(traces_up, onset, start, width), traces_up, 0.0)
    upgoing_spectrum = lax.all_gather(spectra(upgoing, cosine, sine), "rec", axis=3, tiled=True)
    corr_re = jnp.einsum(
        "alt,ath->alh", upgoing_spectrum[0], kernel_real, preferred_element_type=jnp.float32
    ) + jnp.einsum(
        "alt,ath->alh", upgoing_spectrum[1], kernel_imaginary, preferred_element_type=jnp.float32
    )
    corr_im = jnp.einsum(
        "alt,ath->alh", upgoing_spectrum[1], kernel_real, preferred_element_type=jnp.float32
    ) - jnp.einsum(
        "alt,ath->alh", upgoing_spectrum[0], kernel_imaginary, preferred_element_type=jnp.float32
    )
    corr = lax.psum_scatter(jnp.stack([corr_re, corr_im]), "src", scatter_dimension=3, tiled=True)
    reversed_part = synth(corr, rcosine, rsine, samples)
    start_down = (rec_idx * n_src + src_idx) * width
    downgoing = first_arrival - jnp.where(
        onset_masked(reversed_part, onset, start_down, width), reversed_part, 0.0
    )
    return (upgoing, downgoing)


def solution(mesh):
    in_specs = (
        P(None, None, "src", "rec"),
        P(None, ("rec", "src"), None),
        P(None, ("rec", "src"), None),
        P(),
    )
    out_specs = (P(None, ("src", "rec"), None), P(None, ("rec", "src"), None))
    return jax.shard_map(
        per_device, mesh=mesh, in_specs=in_specs, out_specs=out_specs, check_vma=False
    )
```

profile of v0, /device:TPU:32, one launch (start us, length us, event | category | flops | bytes accessed | tf_op | source)
XLA Modules:
  0.0 553.0 jit_solution(9216155911850107133)
XLA Ops:
  7.2 0.7 all-gather.3.cloned.1.call-update
  8.0 59.1 %all-gather.3.cloned.1.call-done = f32[64,256,128]{2,1,0:T(8,128)} async-done(((f32[64,16,128]{2,1,0:T(8,128)}), f32[64,256,128]{2,1,0:T(8,128)}) %all-gather.3.cloned.1.call-update) | async-done | bytes 8388624 | tf_op jit(solution)/shard_map/all_gather | solution.py:47
  67.0 12.0 %negate_convert_fusion = bf16[32,64,256]{2,0,1:T(8,128)(2,1)S(1)} fusion(f32[64,256,128]{2,1,0:T(8,128)} %all-gather.3.cloned.1.call-done, s32[32]{0:T(128)S(1)} %iota_add_fusion), kind=kOutput, calls=%fused_computation.32 | convolution fusion | flops 806412288 | bytes 9437312 | tf_op jit(solution)/shard_map/pnt,kt->kpn/dot_general | solution.py:21
  79.1 1.3 fusion.6
  80.3 8.8 %convolution_convert_fusion = bf16[32,64,256]{2,0,1:T(8,128)(2,1)S(1)} fusion(f32[64,256,128]{2,1,0:T(8,128)S(1)} %copy-done.1, s32[32]{0:T(128)S(1)} %iota_add_fusion), kind=kOutput, calls=%fused_computation.33 | convolution fusion | flops 805888000 | bytes 9437312 | tf_op jit(solution)/shard_map/pnt,kt->kpn/dot_general | solution.py:20
  89.1 1.3 fusion.4
  90.4 1.3 subtract_bitcast_fusion.1
  91.7 1.3 add_bitcast_fusion.1
  93.0 2.3 pad_maximum_fusion
  95.3 9.2 %copy.24 = f32[2,32,64,256]{2,1,0,3:T(8,128)} copy(f32[2,32,64,256]{3,2,1,0:T(8,128)} %pad_maximum_fusion) | data formatting | bytes 8388608 | tf_op jit(solution)/shard_map/stack | solution.py:61
  104.5 0.9 constant_dynamic-slice_fusion
  105.4 224.5 %reduce-scatter.3.cloned.1.call-done = f32[2,32,64,16]{2,1,0,3:T(8,128)} async-done(((f32[2,32,64,256]{2,1,0,3:T(8,128)}), f32[2,32,64,16]{2,1,0,3:T(8,128)}) %reduce-scatter.3.cloned.1.call-update) | async-done | bytes 262160 | tf_op jit(solution)/shard_map/reduce_scatter | solution.py:62
  329.9 1.1 fusion.114
  331.2 0.7 fusion.48
  332.2 0.7 fusion.36
  333.0 1.6 fusion.38
  334.6 1.6 fusion.39
  336.2 0.8 pad_maximum_fusion.2
  337.3 98.7 %all-gather.5.cloned.1.call-done = bf16[2,32,64,256]{2,1,3,0:T(8,128)(2,1)} async-done(((bf16[2,32,64,16]{2,1,3,0:T(8,128)(2,1)}), bf16[2,32,64,256]{2,1,3,0:T(8,128)(2,1)}) %all-gather.5.cloned.1.call-update) | async-done | bytes 2097168 | tf_op jit(solution)/shard_map/all_gather | solution.py:66
  436.0 4.3 slice_bitcast_fusion
  440.3 1.7 copy.30
  441.9 4.4 fusion.2
  446.3 2.8 copy.29
  449.1 3.2 fusion
  452.3 3.2 add_bitcast_fusion
  456.0 0.8 subtract_bitcast_fusion
  456.8 2.3 pad_maximum_fusion.1
  459.1 9.2 %copy.33 = f32[2,32,64,256]{2,1,0,3:T(8,128)} copy(f32[2,32,64,256]{3,2,1,0:T(8,128)} %pad_maximum_fusion.1) | data formatting | bytes 8388608 | tf_op jit(solution)/shard_map/stack | solution.py:77
  468.3 74.3 %reduce-scatter.5.cloned.1.call-done = f32[2,32,64,16]{2,1,0,3:T(8,128)} async-done(((f32[2,32,64,256]{2,1,0,3:T(8,128)}), f32[2,32,64,16]{2,1,0,3:T(8,128)}) %reduce-scatter.5.cloned.1.call-update) | async-done | bytes 262160 | tf_op jit(solution)/shard_map/reduce_scatter | solution.py:77
  542.6 1.1 fusion.113
  544.3 0.7 fusion.45
  545.0 1.5 fusion.34
  (28 shorter events, 2.1 us)
Async XLA Ops:
  7.2 59.8 %all-gather.3.cloned.1.call-start = ((), (), s32[]{:S(2)}) async-start(), calls=%async_computation.2 | async-start | bytes 8912896 | tf_op jit(solution)/shard_map/all_gather | solution.py:47
  7.9 322.0 %reduce-scatter.3.cloned.1.call-start = ((), (), s32[]{:S(2)}) async-start(), calls=%async_computation.3 | async-start | bytes 8912896 | tf_op jit(solution)/shard_map/reduce_scatter | solution.py:62
  67.0 12.0 %copy-start = (bf16[2,32,256,256]{3,2,1,0:T(8,128)(2,1)S(1)}, bf16[2,32,256,256]{3,2,1,0:T(8,128)(2,1)}, u32[]{:S(2)}) copy-start(bf16[2,32,256,256]{3,2,1,0:T(8,128)(2,1)} %param.4) | copy-start | bytes 25165828
  67.0 13.3 %copy-start.1 = (f32[64,256,128]{2,1,0:T(8,128)S(1)}, f32[64,256,128]{2,1,0:T(8,128)}, u32[]{:S(2)}) copy-start(f32[64,256,128]{2,1,0:T(8,128)} %all-gather.3.cloned.1.call-done) | copy-start | bytes 25165828
  104.5 331.5 %all-gather.5.cloned.1.call-start = ((), (), s32[]{:S(2)}) async-start(), calls=%async_computation.4 | async-start | bytes 4456448 | tf_op jit(solution)/shard_map/all_gather | solution.py:66
  332.9 1.7 copy-start.3
  337.0 205.6 %reduce-scatter.5.cloned.1.call-start = ((), (), s32[]{:S(2)}) async-start(), calls=%async_computation.5 | async-start | bytes 8912896 | tf_op jit(solution)/shard_map/reduce_scatter | solution.py:77
  449.1 3.2 copy-start.2
  449.1 6.4 %slice-start = ((s8[8388608]{0:T(1024)(128)(4,1)}), s8[4194304]{0:T(1024)(128)(4,1)S(1)}, s32[]{:S(2)}) async-start(s8[8388608]{0:T(1024)(128)(4,1)} %bitcast.80), calls=%async_computation.6 | async-start | bytes 8388608
  452.3 3.7 slice-start.1
  468.2 76.7 %copy-start.4 = (f32[64,16,128]{2,1,0:T(8,128)S(1)}, f32[64,16,128]{2,1,0:T(8,128)}, u32[]{:S(2)}) copy-start(f32[64,16,128]{2,1,0:T(8,128)} %param.6) | copy-start | bytes 1572868
Sparse Core Ops, SparseCore 0:
  9.8 57.1 all-gather.2
  104.6 225.2 reduce-scatter.2
  337.2 98.7 all-gather.4
  468.4 74.1 reduce-scatter.4
where the time goes:
time: 554 us; the launch traced here: 553 us
  waiting for transfers between devices  457 us (82%)
  matrix products  44.4 us (8%)
  local copies, waits for them, and re-layouts  31.7 us (6%)
  between operations  14 us (3%)
    reduce_scatter x1, waiting for transfers between devices, per_device(): share = lax.psum_scatter(conv, 'rec', scatter_dimension=3, tiled=True)  224 us
    all_gather x1, waiting for transfers between devices, per_device(): lax.all_gather(spectra(upgoing, cosine, sine), 'rec', axis=3, tiled=True)  98.7 us
    reduce_scatter x1, waiting for transfers between devices, per_device(): lax.psum_scatter(jnp.stack([corr_re, corr_im]), 'src', scatter_dimension=...  74.3 us
    all_gather x1, waiting for transfers between devices, per_device(): traces = lax.all_gather(focusing, 'src', axis=1, tiled=True)  59.1 us
    dot_general x2, matrix products, spectra(): imag_part = -jnp.einsum('pnt,kt->kpn', traces, sine, precision=HIGH)  13.7 us
  transfers between devices with their start and end apart: 4, of which 4 were waited for; matrix products, arithmetic and copies ran while one was open for 0% of the time, Pallas kernels for 0%

commit v1 on v0

--- a/solution.py
+++ b/solution.py
@@ -63,7 +63,11 @@
     start = (src_idx * n_rec + rec_idx) * width
     traces_up = synth(share, cosine, sine, samples)
     upgoing = jnp.where(onset_masked(traces_up, onset, start, width), traces_up, 0.0)
-    upgoing_spectrum = lax.all_gather(spectra(upgoing, cosine, sine), "rec", axis=3, tiled=True)
+    x = spectra(upgoing, cosine, sine)
+    size = lax.axis_size("rec")
+    blocks = jnp.stack([x for _ in range(size)])
+    blocks = lax.all_to_all(blocks, "rec", split_axis=0, concat_axis=0)
+    upgoing_spectrum = jnp.concatenate(blocks, axis=3)
     corr_re = jnp.einsum(
         "alt,ath->alh", upgoing_spectrum[0], kernel_real, preferred_element_type=jnp.float32
     ) + jnp.einsum(

time: 554 us -> 512 us (0.924)
  waiting for transfers between devices: 457 us -> 359 us
  blocking collectives: 0 us -> 52.5 us
  local copies, waits for them, and re-layouts: 31.7 us -> 45.1 us
  matrix products: 44.4 us -> 36.3 us
    all_gather x1 -> x0, waiting for transfers between devices: 98.7 us -> none  [per_device(): lax.all_gather(spectra(upgoing, cosine, sine), 'rec', axis=3, tiled=True)]
    all_to_all x0 -> x1, blocking collectives: none -> 52.5 us  [per_device(): blocks = lax.all_to_all(blocks, 'rec', split_axis=0, concat_axis=0)]
    unnamed x18 -> x19, local copies, waits for them, and re-layouts: 1.64 us -> 18.3 us
    squeeze x3 -> x0, local copies, waits for them, and re-layouts: 8.76 us -> none  [the longest x2 5.97 us: per_device(): upgoing_spectrum[1]]
  transfers between devices with their start and end apart: 4 -> 3, of which waited for: 4 -> 3; matrix products, arithmetic and copies ran while one was open for 0% -> 0% of each run, Pallas kernels for 0% -> 0%
where the time goes in v1:
time: 512 us
  waiting for transfers between devices  359 us (70%)
  blocking collectives  52.5 us (10%)
  local copies, waits for them, and re-layouts  45.1 us (9%)
  matrix products  36.3 us (7%)
  between operations  14 us (3%)
    reduce_scatter x1, waiting for transfers between devices, per_device(): share = lax.psum_scatter(conv, 'rec', scatter_dimension=3, tiled=True)  224 us
    reduce_scatter x1, waiting for transfers between devices, per_device(): lax.psum_scatter(jnp.stack([corr_re, corr_im]), 'src', scatter_dimension=...  74.8 us
    all_gather x1, waiting for transfers between devices, per_device(): traces = lax.all_gather(focusing, 'src', axis=1, tiled=True)  59.1 us
    all_to_all x1, blocking collectives, per_device(): blocks = lax.all_to_all(blocks, 'rec', split_axis=0, concat_axis=0)  52.5 us
    unnamed x19, local copies, waits for them, and re-layouts  18.3 us
    dot_general x2, matrix products, spectra(): imag_part = -jnp.einsum('pnt,kt->kpn', traces, sine, precision=HIGH)  13.7 us
    dot_general x2, matrix products, spectra(): real_part = jnp.einsum('pnt,kt->kpn', traces, cosine, precision=HIGH)  10.4 us
  transfers between devices with their start and end apart: 3, of which 3 were waited for; matrix products, arithmetic and copies ran while one was open for 0% of the time, Pallas kernels for 0%

profile of v1, /device:TPU:32, one launch (start us, length us, event | category | flops | bytes accessed | tf_op | source)
XLA Modules:
  0.0 511.6 jit_solution(7807059555065580149)
XLA Ops:
  8.0 59.1 %all-gather.2.cloned.1.call-done = f32[64,256,128]{2,1,0:T(8,128)} async-done(((f32[64,16,128]{2,1,0:T(8,128)}), f32[64,256,128]{2,1,0:T(8,128)}) %all-gather.2.cloned.1.call-update) | async-done | bytes 8388624 | tf_op jit(solution)/shard_map/all_gather | solution.py:47
  67.0 12.0 %negate_convert_fusion = bf16[32,64,256]{2,0,1:T(8,128)(2,1)S(1)} fusion(f32[64,256,128]{2,1,0:T(8,128)} %all-gather.2.cloned.1.call-done, s32[32]{0:T(128)S(1)} %iota_add_fusion), kind=kOutput, calls=%fused_computation.30 | convolution fusion | flops 806412288 | bytes 9437312 | tf_op jit(solution)/shard_map/pnt,kt->kpn/dot_general | solution.py:21
  79.1 1.3 fusion.6
  80.3 8.8 %convolution_convert_fusion = bf16[32,64,256]{2,0,1:T(8,128)(2,1)S(1)} fusion(f32[64,256,128]{2,1,0:T(8,128)S(1)} %copy-done.1, s32[32]{0:T(128)S(1)} %iota_add_fusion), kind=kOutput, calls=%fused_computation.31 | convolution fusion | flops 805888000 | bytes 9437312 | tf_op jit(solution)/shard_map/pnt,kt->kpn/dot_general | solution.py:20
  89.1 1.3 fusion.4
  90.4 1.3 subtract_bitcast_fusion.1
  91.7 1.3 add_bitcast_fusion.1
  93.0 2.2 pad_maximum_fusion
  95.3 9.2 %copy.36 = f32[2,32,64,256]{2,1,0,3:T(8,128)} copy(f32[2,32,64,256]{3,2,1,0:T(8,128)} %pad_maximum_fusion) | data formatting | bytes 8388608 | tf_op jit(solution)/shard_map/stack | solution.py:61
  104.5 0.9 constant_dynamic-slice_fusion
  105.4 224.5 %reduce-scatter.3.cloned.1.call-done = f32[2,32,64,16]{2,1,0,3:T(8,128)} async-done(((f32[2,32,64,256]{2,1,0,3:T(8,128)}), f32[2,32,64,16]{2,1,0,3:T(8,128)}) %reduce-scatter.3.cloned.1.call-update) | async-done | bytes 262160 | tf_op jit(solution)/shard_map/reduce_scatter | solution.py:62
  329.8 1.1 fusion.115
  331.2 0.7 fusion.48
  332.2 0.7 fusion.36
  332.9 1.6 fusion.38
  334.6 1.6 fusion.39
  336.4 2.9 broadcast_bitcast_fusion
  339.3 6.3 %reshape.40 = bf16[16,2,32768]{2,1,0:T(2,128)(2,1)S(1)} reshape(bf16[16,2,32,16,64]{4,3,2,1,0:T(8,128)(2,1)} %broadcast_bitcast_fusion) | data formatting | bytes 4194304
  345.6 52.5 %all_to_all.5 = bf16[16,2,32768]{2,1,0:T(2,128)(2,1)} all-to-all(bf16[16,2,32768]{2,1,0:T(2,128)(2,1)S(1)} %reshape.40), channel_id=1, replica_groups=mesh['src'=16,'rec'=16] {'rec'}, dimensions={0} | all-to-all | bytes 4194304 | tf_op jit(solution)/shard_map/all_to_all | solution.py:69
  398.2 7.4 %reshape.41 = bf16[16,2,32,16,64]{4,3,2,1,0:T(8,128)(2,1)} reshape(bf16[16,2,32768]{2,1,0:T(2,128)(2,1)} %all_to_all.5) | data formatting | bytes 4194304
  405.5 3.1 bitcast_bitcast_fusion
  408.7 1.1 fusion.113
  410.9 0.8 fusion.2
  412.4 0.8 fusion
  413.2 0.9 add_bitcast_fusion
  414.1 0.9 subtract_bitcast_fusion
  415.0 2.2 pad_maximum_fusion.1
  417.2 9.2 %copy.48 = f32[2,32,64,256]{2,1,0,3:T(8,128)} copy(f32[2,32,64,256]{3,2,1,0:T(8,128)} %pad_maximum_fusion.1) | data formatting | bytes 8388608 | tf_op jit(solution)/shard_map/stack | solution.py:81
  426.4 74.8 %reduce-scatter.5.cloned.1.call-done = f32[2,32,64,16]{2,1,0,3:T(8,128)} async-done(((f32[2,32,64,256]{2,1,0,3:T(8,128)}), f32[2,32,64,16]{2,1,0,3:T(8,128)}) %reduce-scatter.5.cloned.1.call-update) | async-done | bytes 262160 | tf_op jit(solution)/shard_map/reduce_scatter | solution.py:81
  501.2 1.1 fusion.114
  502.9 0.7 fusion.45
  503.6 1.5 fusion.34
  (29 shorter events, 3.8 us)
Async XLA Ops:
  7.2 59.8 %all-gather.2.cloned.1.call-start = ((), (), s32[]{:S(2)}) async-start(), calls=%async_computation.3 | async-start | bytes 8912896 | tf_op jit(solution)/shard_map/all_gather | solution.py:47
  7.9 322.0 %reduce-scatter.3.cloned.1.call-start = ((), (), s32[]{:S(2)}) async-start(), calls=%async_computation.4 | async-start | bytes 8912896 | tf_op jit(solution)/shard_map/reduce_scatter | solution.py:62
  67.0 12.0 %copy-start = (bf16[2,32,256,256]{3,2,1,0:T(8,128)(2,1)S(1)}, bf16[2,32,256,256]{3,2,1,0:T(8,128)(2,1)}, u32[]{:S(2)}) copy-start(bf16[2,32,256,256]{3,2,1,0:T(8,128)(2,1)} %param.4) | copy-start | bytes 25165828
  67.0 13.3 %copy-start.1 = (f32[64,256,128]{2,1,0:T(8,128)S(1)}, f32[64,256,128]{2,1,0:T(8,128)}, u32[]{:S(2)}) copy-start(f32[64,256,128]{2,1,0:T(8,128)} %all-gather.2.cloned.1.call-done) | copy-start | bytes 25165828
  104.5 396.8 %reduce-scatter.5.cloned.1.call-start = ((), (), s32[]{:S(2)}) async-start(), calls=%async_computation.5 | async-start | bytes 8912896 | tf_op jit(solution)/shard_map/reduce_scatter | solution.py:81
  332.9 12.7 %copy-start.2 = (f32[64,16,128]{2,1,0:T(8,128)}, f32[64,16,128]{2,1,0:T(8,128)S(1)}, u32[]{:S(2)}) copy-start(f32[64,16,128]{2,1,0:T(8,128)S(1)} %fusion.36) | copy-start | bytes 1572868
  405.5 4.9 slice-start
  408.7 2.3 slice-start.1
  426.3 77.2 %copy-start.3 = (f32[64,16,128]{2,1,0:T(8,128)S(1)}, f32[64,16,128]{2,1,0:T(8,128)}, u32[]{:S(2)}) copy-start(f32[64,16,128]{2,1,0:T(8,128)} %param.6) | copy-start | bytes 1572868
Sparse Core Ops, SparseCore 0:
  9.8 57.1 all-gather.1
  104.6 225.2 reduce-scatter.2
  426.5 74.6 reduce-scatter.4
